TPU v7x, 32 devices: a whole 2x2x4 slice. The times are simulated.
32 devices in a mesh: chan: 4 (over y, x), space: 4 (over z), rep: 2 (over core).
Axes of the slice: x: 2, y: 2, z: 4, core: 2. Of those that a mesh axis runs over, the one named last changes fastest.
Arguments:
- inputs: bfloat16 [2, 2, 16, 512, 128], P('rep', None, 'space', 'chan'), may hold values from -6 to 6
- grad_out: bfloat16 [2, 2, 16, 512, 128], P('rep', None, 'space', 'chan'), may hold values from -6 to 6
- weight: bfloat16 [3, 3, 3, 512, 512], P(None, None, None, 'chan'), may hold values from -0.0546875 to 0.0546875
Outputs:
- grad_in: bfloat16 [2, 2, 16, 512, 128], P('rep', None, 'space', 'chan')
- grad_weight: float32 [3, 3, 3, 512, 512], P(None, None, None, ('chan', 'rep'))
All inputs are finite; a program needn't handle non-finite values.
Results may differ from a plain program's by a relative error of at most 0.0031.
Values may be sent and summed in bfloat16 or wider, within the bound.
A program may use at most 64 MiB of HBM per device.

v0:
```python
import jax
import jax.numpy as jnp
from jax import lax
from jax.sharding import PartitionSpec as P


def with_halo(cells, sides, width):
    for axis, dim in sides:
        count = lax.axis_size(axis)
        ends = count - 1
        head = lax.slice_in_dim(cells, 0, width, axis=dim)
        tail = lax.slice_in_dim(cells, cells.shape[dim] - width, cells.shape[dim], axis=dim)
        cells = jnp.concatenate(
            [
                lax.ppermute(tail, axis, [(i, (i + 1) % count) for i in range(ends)]),
                cells,
                lax.ppermute(head, axis, [((i + 1) % count, i) for i in range(ends)]),
            ],
            axis=dim,
        )
    return cells


def silu_slope(values):
    logistic = jax.nn.sigmoid(values)
    return logistic * (1.0 + values * (1.0 - logistic))


def tap_windows(padded, frame_count, row_count, col_count):
    windows = []
    for frame_tap in range(3):
        for row_tap in range(3):
            for col_tap in range(3):
                windows.append(
                    padded[
                        :,
                        2 - frame_tap : 2 - frame_tap + frame_count,
                        2 - row_tap : 2 - row_tap + row_count,
                        :,
                        2 - col_tap : 2 - col_tap + col_count,
                    ]
                )
    return jnp.concatenate(windows, axis=3)


def on_device(inputs, grad_out, weight):
    clip_count, frame_count, row_count, in_part, col_count = inputs.shape
    out_part = grad_out.shape[3]
    gathered = lax.all_gather(inputs, "chan", axis=3, tiled=True)
    activated = jax.nn.silu(gathered.astype(jnp.float32)).astype(jnp.bfloat16)
    in_width = activated.shape[3]
    grad_rim = with_halo(grad_out, (("space", 2),), 1)
    grad_pad = jnp.pad(grad_rim, ((0, 0), (0, 2), (0, 0), (0, 0), (1, 1)))
    stacked = tap_windows(grad_pad, frame_count, row_count, col_count)
    local_flat = jnp.einsum(
        "cthkw,cthiw->ki", stacked, activated, preferred_element_type=jnp.float32
    )
    local_weight = local_flat.reshape(3, 3, 3, out_part, in_width)
    clip_summed = lax.psum_scatter(local_weight, "rep", scatter_dimension=3, tiled=True)
    summed = lax.psum(clip_summed, "space")
    grad_weight = summed * (1.0 / 256.0)
    flat_kernel = weight.reshape(27 * out_part, weight.shape[4])
    partial_value = jnp.einsum(
        "cthkw,ki->cthiw", stacked, flat_kernel, preferred_element_type=jnp.float32
    )
    active_grad = lax.psum_scatter(partial_value, "chan", scatter_dimension=3, tiled=True)
    grad_in = (active_grad * silu_slope(inputs.astype(jnp.float32))).astype(jnp.bfloat16)
    return (grad_in, grad_weight)


def solution(mesh):
    return jax.shard_map(
        on_device,
        mesh=mesh,
        in_specs=(
            P("rep", None, "space", "chan", None),
            P("rep", None, "space", "chan", None),
            P(None, None, None, "chan", None),
        ),
        out_specs=(
            P("rep", None, "space", "chan", None),
            P(None, None, None, ("chan", "rep"), None),
        ),
        check_vma=False,
    )
```

profile of v0, /device:TPU:0, one launch (start us, length us, event | category | flops | bytes accessed | tf_op | source)
XLA Modules:
  0.0 258.9 jit_solution(6788880601391279087)
XLA Ops:
  7.2 1.9 copy.15
  9.2 1.5 fusion.32
  10.7 1.3 collective-permute-start.1
  12.0 6.2 %collective-permute-start = (bf16[1,2,1,128,128]{3,4,2,1,0:T(8,128)(2,1)}, bf16[1,2,1,128,128]{3,4,2,1,0:T(8,128)(2,1)}, u32[]{:S(2)}, u32[]{:S(2)}) collective-permute-start(bf16[1,2,1,128,128]{3,4,2,1,0:T(8,128)(2,1)} %get-tuple-element.6), channel_id=1, source_target_pairs={{0,2},{2,4},{4,6},{1,3},{3,5},{5,7},{8,10},{10,12},{12,14},{9,11},... | collective-permute-start | bytes 196616 | tf_op jit(solution)/shard_map/ppermute | solution.py:15
  19.1 0.6 collective-permute-done
  19.7 1.2 fusion.20
  20.9 0.1 slice_dynamic-update-slice_fusion.14
  21.3 0.1 slice_dynamic-update-slice_fusion.10
  21.6 0.1 slice_dynamic-update-slice_fusion.8
  22.0 0.9 fusion.31
  23.4 0.9 fusion.30
  24.4 2.9 %copy-done.2 = bf16[1,2,4,3456,128]{3,4,2,1,0:T(8,128)(2,1)} copy-done((bf16[1,2,4,3456,128]{3,4,2,1,0:T(8,128)(2,1)}, bf16[1,2,4,3456,128]{3,4,2,1,0:T(8,128)(2,1)S(1)}, u32[]{:S(2)}) %copy-start.2) | copy-done | bytes 7077912
  27.3 10.2 %copy.22 = bf16[3456,4,2,128]{3,0,2,1:T(8,128)(2,1)} copy(bf16[3456,4,2,128]{0,3,1,2:T(8,128)(2,1)} %bitcast.31) | data formatting | bytes 14155776 | tf_op jit(solution)/shard_map/cthkw,cthiw->ki/dot_general | solution.py:55
  37.5 8.1 %all-gather.2.cloned.1.call-done = bf16[1,2,4,512,128]{4,3,2,1,0:T(8,128)(2,1)} async-done(((bf16[1,2,4,128,128]{4,3,2,1,0:T(8,128)(2,1)}), bf16[1,2,4,512,128]{4,3,2,1,0:T(8,128)(2,1)}) %all-gather.2.cloned.1.call-update) | async-done | bytes 1048592 | tf_op jit(solution)/shard_map/all_gather | solution.py:49
  45.6 6.6 %fusion = f32[3,3,3,128,512,1,1]{4,3,0,1,2,6,5:T(8,128)S(1)} fusion(bf16[3,3,3,128,4,2,128]{6,3,2,1,0,5,4:T(8,128)(2,1)} %bitcast.32, bf16[1,2,4,512,128]{4,3,2,1,0:T(8,128)(2,1)} %all-gather.2.cloned.1.call-done), kind=kOutput, calls=%fused_computation | convolution fusion | flops 3627024384 | bytes 15204352 | tf_op jit(solution)/shard_map/cthkw,cthiw->ki/dot_general | solution.py:55
  52.3 3.7 %copy.38 = f32[3,3,3,128,512,1,1]{4,3,2,1,0,5,6:T(8,128)} copy(f32[3,3,3,128,512,1,1]{4,3,0,1,2,6,5:T(8,128)S(1)} %fusion) | data formatting | bytes 14155776 | tf_op jit(solution)/shard_map/cthkw,cthiw->ki/dot_general | solution.py:55
  56.1 7.5 %fusion.13 = f32[1,2,4,512,128]{3,4,2,1,0:T(8,128)} fusion(bf16[3456,512,1,1]{1,0,3,2:T(8,128)(2,1)S(1)} %bitcast.29, bf16[1,2,4,3456,128]{3,4,2,1,0:T(8,128)(2,1)} %copy-done.2), kind=kOutput, calls=%fused_computation.20 | convolution fusion | flops 3623878656 | bytes 12713984 | tf_op jit(solution)/shard_map/cthkw,ki->cthiw/dot_general | solution.py:63
  63.7 7.9 %reduce-scatter.5.cloned.1.call-done = f32[3,3,3,64,512]{4,3,2,1,0:T(8,128)} async-done(((f32[3,3,3,128,512]{4,3,2,1,0:T(8,128)}), f32[3,3,3,64,512]{4,3,2,1,0:T(8,128)}) %reduce-scatter.5.cloned.1.call-update) | async-done | bytes 3538960 | tf_op jit(solution)/shard_map/reduce_scatter | solution.py:59
  71.7 1.8 copy.21
  73.5 38.5 %reduce-scatter.3.cloned.1.call-done = f32[1,2,4,128,128]{3,4,2,1,0:T(8,128)} async-done(((f32[1,2,4,512,128]{3,4,2,1,0:T(8,128)}), f32[1,2,4,128,128]{3,4,2,1,0:T(8,128)}) %reduce-scatter.3.cloned.1.call-update) | async-done | bytes 524304 | tf_op jit(solution)/shard_map/reduce_scatter | solution.py:66
  111.9 2.0 fusion.29
  113.9 1.8 copy.25
  115.7 132.2 %all-reduce.3.cloned.1.call-done = f32[3,3,3,64,512]{4,3,2,1,0:T(8,128)} async-done(((f32[3,3,3,64,512]{4,3,2,1,0:T(8,128)}), f32[3,3,3,64,512]{4,3,2,1,0:T(8,128)}) %all-reduce.3.cloned.1.call-update) | async-done | bytes 3538960 | tf_op jit(solution)/shard_map/psum | solution.py:60
  248.0 4.4 %broadcast_multiply_fusion = f32[3,3,3,64,512]{4,3,2,1,0:T(8,128)} fusion(f32[3,3,3,64,512]{4,3,2,1,0:T(8,128)} %all-reduce.3.cloned.1.call-done), kind=kLoop, calls=%fused_computation.13 | loop fusion | flops 884736 | bytes 7077888 | tf_op jit(solution)/shard_map/mul | solution.py:61
  (36 shorter events, 2.2 us)
Async XLA Ops:
  7.2 48.9 %copy-start = (bf16[3,3,3,128,512]{4,3,2,1,0:T(8,128)(2,1)S(1)}, bf16[3,3,3,128,512]{4,3,2,1,0:T(8,128)(2,1)}, u32[]{:S(2)}) copy-start(bf16[3,3,3,128,512]{4,3,2,1,0:T(8,128)(2,1)} %param.5) | copy-start | bytes 10616836
  7.2 38.5 %all-gather.2.cloned.1.call-start = ((), (), s32[]{:S(2)}) async-start(), calls=%async_computation.3 | async-start | bytes 1310720 | tf_op jit(solution)/shard_map/all_gather | solution.py:49
  10.7 8.5 %collective-permute-start.1 = (bf16[1,2,1,128,128]{3,4,2,1,0:T(8,128)(2,1)}, bf16[1,2,1,128,128]{3,4,2,1,0:T(8,128)(2,1)}, u32[]{:S(2)}, u32[]{:S(2)}) collective-permute-start(bf16[1,2,1,128,128]{3,4,2,1,0:T(8,128)(2,1)} %get-tuple-element.7), channel_id=1, source_target_pairs={{2,0},{4,2},{6,4},{3,1},{5,3},{7,5},{10,8},{12,10},{14,12},{11,9},... | collective-permute-start | bytes 196616 | tf_op jit(solution)/shard_map/ppermute | solution.py:17
  12.0 7.8 %collective-permute-start = (bf16[1,2,1,128,128]{3,4,2,1,0:T(8,128)(2,1)}, bf16[1,2,1,128,128]{3,4,2,1,0:T(8,128)(2,1)}, u32[]{:S(2)}, u32[]{:S(2)}) collective-permute-start(bf16[1,2,1,128,128]{3,4,2,1,0:T(8,128)(2,1)} %get-tuple-element.6), channel_id=1, source_target_pairs={{0,2},{2,4},{4,6},{1,3},{3,5},{5,7},{8,10},{10,12},{12,14},{9,11},... | collective-permute-start | bytes 196616 | tf_op jit(solution)/shard_map/ppermute | solution.py:15
  18.2 53.4 %reduce-scatter.5.cloned.1.call-start = ((), (), s32[]{:S(2)}) async-start(), calls=%async_computation.4 | async-start | bytes 10616832 | tf_op jit(solution)/shard_map/reduce_scatter | solution.py:59
  18.2 3.8 %copy-start.1 = (bf16[1,2,4,128,128]{3,4,2,1,0:T(8,128)(2,1)S(1)}, bf16[1,2,4,128,128]{3,4,2,1,0:T(8,128)(2,1)}, u32[]{:S(2)}) copy-start(bf16[1,2,4,128,128]{3,4,2,1,0:T(8,128)(2,1)} %copy.15) | copy-start | bytes 786436
  24.4 2.9 %copy-start.2 = (bf16[1,2,4,3456,128]{3,4,2,1,0:T(8,128)(2,1)}, bf16[1,2,4,3456,128]{3,4,2,1,0:T(8,128)(2,1)S(1)}, u32[]{:S(2)}) copy-start(bf16[1,2,4,3456,128]{3,4,2,1,0:T(8,128)(2,1)S(1)} %slice_dynamic-update-slice_fusion) | copy-start | bytes 21233668
  56.0 55.9 %reduce-scatter.3.cloned.1.call-start = ((), (), s32[]{:S(2)}) async-start(), calls=%async_computation.2 | async-start | bytes 2621440 | tf_op jit(solution)/shard_map/reduce_scatter | solution.py:66
  63.7 184.3 %all-reduce.3.cloned.1.call-start = ((), (), s32[]{:S(2)}) async-start(), calls=%async_computation.5 | async-start | bytes 7077888 | tf_op jit(solution)/shard_map/psum | solution.py:60
Sparse Core Ops, SparseCore 0:
  18.3 27.2 all-gather.1
  56.2 15.4 reduce-scatter.4
  75.5 36.4 reduce-scatter.2
  114.2 133.7 all-reduce.2
where the time goes:
time: 260 us; the launch traced here: 259 us
  waiting for transfers between devices  187 us (72%)
  local copies, waits for them, and re-layouts  26.3 us (10%)
  matrix products  14.2 us (5%)
  between operations  14 us (5%)
  other arithmetic  9.39 us (4%)
  starting transfers between devices  7.63 us (3%)
    psum x1, waiting for transfers between devices, on_device(): summed = lax.psum(clip_summed, 'space')  132 us
    reduce_scatter x1, waiting for transfers between devices, on_device(): lax.psum_scatter(partial_value, 'chan', scatter_dimension=3, tiled=True)  38.5 us
    dot_general x2, local copies, waits for them, and re-layouts, on_device(): jnp.einsum('cthkw,cthiw->ki', stacked, activated, preferred_element_type=...  14 us
    unnamed x33, local copies, waits for them, and re-layouts  10.7 us
    all_gather x1, waiting for transfers between devices, on_device(): gathered = lax.all_gather(inputs, 'chan', axis=3, tiled=True)  8.09 us
    reduce_scatter x1, waiting for transfers between devices, on_device(): lax.psum_scatter(local_weight, 'rep', scatter_dimension=3, tiled=True)  7.92 us
    dot_general x1, matrix products, on_device(): jnp.einsum('cthkw,ki->cthiw', stacked, flat_kernel, preferred_element_typ...  7.54 us
    dot_general x1, matrix products, on_device(): jnp.einsum('cthkw,cthiw->ki', stacked, activated, preferred_element_type=...  6.64 us
  transfers between devices with their start and end apart: 6, of which 5 were waited for; matrix products, arithmetic and copies ran while one was open for 11% of the time, Pallas kernels for 0%

commit v1 on v0

v1 whole, which is shorter than its diff:
```python
import functools

import jax
import jax.numpy as jnp
from jax import lax
from jax.experimental import pallas as pl
from jax.experimental.pallas import tpu as pltpu
from jax.sharding import PartitionSpec as P

MESH = pl.DeviceIdType.MESH
F32 = jnp.float32
BF16 = jnp.bfloat16
LANES = 128


def flip(index, mask, count):
    out, bit = 0, 1
    while bit < count:
        out = out + (((index // bit) + ((mask // bit) % 2)) % 2) * bit
        bit *= 2
    return out


def nt(a, b):
    return lax.dot_general(a, b, (((1,), (1,)), ((), ())), preferred_element_type=F32)


def tn(a, b):
    return lax.dot_general(a, b, (((0,), (0,)), ((), ())), preferred_element_type=F32)


def kernel(
    cfg,
    x_ref, g_ref, w_hbm,
    gi_ref, gw_ref,
    act, halo_top, halo_bot, sib_top, sib_bot, sib_rows,
    xd, xw, w_ref, part, right_buf, left_buf, total,
    d_acc, d_send, d_recv,
    w_sem, g_send, g_recv, a_send, a_recv, b_send, b_recv,
    r_send, r_recv, l_send, l_recv, fr_send, fl_send, f_recv, d_ssem, d_rsem,
):
    n_c, n_s, frames, rows, in_part, out_part, cols, in_all = cfg
    half = out_part // 2
    first = max(0, 3 - frames)
    taps = 3 - first
    plane = rows * cols
    cells = frames * plane
    width = max(LANES, in_part)
    blocks = in_all // width
    per = width // in_part
    grad_rows = taps * 9 * half
    own_count = max(n for n in range(1, n_s + 1) if grad_rows % (16 * n) == 0)
    piece = grad_rows // own_count

    chan = lax.axis_index("chan")
    space = lax.axis_index("space")
    rep = lax.axis_index("rep")
    other = 1 - rep
    has_left = space > 0
    has_right = space < n_s - 1
    after = (space + 1) % n_s
    before = (space + n_s - 1) % n_s

    def remote(src, dst, ssem, rsem, **where):
        return pltpu.make_async_remote_copy(
            src_ref=src, dst_ref=dst, send_sem=ssem, recv_sem=rsem,
            device_id=where, device_id_type=MESH,
        )

    weight_copy = pltpu.make_async_copy(
        w_hbm.at[pl.ds(first * 9 * out_part, taps * 9 * out_part)], w_ref, w_sem
    )
    weight_copy.start()

    barrier = pltpu.get_barrier_semaphore()

    def greet(**where):
        pl.semaphore_signal(barrier, inc=1, device_id=where, device_id_type=MESH)

    for k in range(1, n_c):
        greet(chan=flip(chan, k, n_c))
    greet(rep=other)

    @pl.when(has_left)
    def _():
        greet(space=before)
        greet(space=before, rep=other)

    @pl.when(has_right)
    def _():
        greet(space=after)
        greet(space=after, rep=other)

    my_rows = pl.ds(pl.multiple_of(chan * in_part, in_part), in_part)
    for t in range(frames):
        for h in range(rows):
            v = x_ref[t, h].astype(F32)
            at = (t * rows + h) * cols
            act[0, my_rows, at : at + cols] = (v * jax.nn.sigmoid(v)).astype(BF16)

    inner = jnp.logical_and(has_left, has_right)

    @pl.when(inner)
    def _():
        pl.semaphore_wait(barrier, n_c + 4)

    @pl.when(jnp.logical_not(inner))
    def _():
        pl.semaphore_wait(barrier, n_c + (2 if n_s > 1 else 0))

    theirs = pl.ds(pl.multiple_of(other * half, half), half)

    def down():
        return remote(g_ref.at[:, rows - 1], halo_top, g_send.at[0], g_recv.at[0], space=after)

    def down_sib():
        return remote(g_ref.at[:, rows - 1, theirs], sib_top, g_send.at[1], g_recv.at[1], space=after, rep=other)

    def up():
        return remote(g_ref.at[:, 0], halo_bot, g_send.at[2], g_recv.at[2], space=before)

    def up_sib():
        return remote(g_ref.at[:, 0, theirs], sib_bot, g_send.at[3], g_recv.at[3], space=before, rep=other)

    def across():
        return remote(g_ref.at[:, :, theirs], sib_rows, g_send.at[4], g_recv.at[4], rep=other)

    @pl.when(has_right)
    def _():
        down().start()
        down_sib().start()

    @pl.when(has_left)
    def _():
        up().start()
        up_sib().start()

    across().start()

    def chan_rows(k):
        owner = flip(chan, k, n_c)
        return pl.ds(pl.multiple_of(owner * in_part, in_part), in_part)

    def relay(k):
        return remote(act.at[0, chan_rows(k)], act.at[1, chan_rows(k)], b_send.at[k], b_recv.at[k], rep=other)

    def spread(k):
        return remote(act.at[0, my_rows], act.at[0, my_rows], a_send.at[k], a_recv.at[k], chan=flip(chan, k, n_c))

    relay(0).start()
    for k in range(1, n_c):
        spread(k).start()

    @pl.when(has_left)
    def _():
        down().wait_recv()
        down_sib().wait_recv()

    @pl.when(jnp.logical_not(has_left))
    def _():
        halo_top[...] = jnp.zeros_like(halo_top)
        sib_top[...] = jnp.zeros_like(sib_top)

    @pl.when(has_right)
    def _():
        up().wait_recv()
        up_sib().wait_recv()

    @pl.when(jnp.logical_not(has_right))
    def _():
        halo_bot[...] = jnp.zeros_like(halo_bot)
        sib_bot[...] = jnp.zeros_like(sib_bot)

    across().wait_recv()

    def shifts(row):
        v = row.astype(F32)
        lane = lax.broadcasted_iota(jnp.int32, v.shape, 1)
        ahead = jnp.where(lane < cols - 1, pltpu.roll(v, cols - 1, 1), 0.0)
        behind = jnp.where(lane > 0, pltpu.roll(v, 1, 1), 0.0)
        return ahead.astype(BF16), row, behind.astype(BF16)

    def lay(dst, top, bottom, middle):
        for t in range(frames):
            for p in range(rows + 2):
                row = top(t) if p == 0 else bottom(t) if p == rows + 1 else middle(t, p - 1)
                moved = shifts(row)
                for b in range(3):
                    h = p + b - 2
                    if 0 <= h < rows:
                        at = (t * rows + h) * cols
                        for e in range(3):
                            dst(b * 3 + e, at, moved[e])

    def to_sib(i, at, value):
        xw[1, i * half : (i + 1) * half, at : at + cols] = value

    def to_own(i, at, value):
        xd[i * out_part : (i + 1) * out_part, at : at + cols] = value

    lay(to_sib, lambda t: sib_top[t], lambda t: sib_bot[t], lambda t, h: sib_rows[t, h])
    lay(to_own, lambda t: halo_top[t], lambda t: halo_bot[t], lambda t, h: g_ref[t, h])
    for i in range(9):
        xw[0, i * half : (i + 1) * half, :] = xd[
            pl.ds(pl.multiple_of(i * out_part + rep * half, half), half), :
        ]

    def block_of(j):
        return flip(chan // per, j, blocks)

    def kernel_grad(j):
        where = pl.ds(pl.multiple_of(block_of(j) * width, width), width)
        for a in range(first, 3):
            skip, used = (2 - a) * plane, (frames - 2 + a) * plane
            value = nt(xw[0, :, skip:cells], act[0, where, 0:used])
            value = value + nt(xw[1, :, skip:cells], act[1, where, 0:used])
            at = (a - first) * 9 * half
            part[j, at : at + 9 * half, :] = value

    def fetch(j):
        for k in range(j * per, (j + 1) * per):
            if k:
                spread(k).wait_recv()
                relay(k).start()

    def settle(j):
        for k in range(j * per, (j + 1) * per):
            relay(k).wait_recv()

    def rows_of(q):
        return pl.ds(pl.multiple_of(q * piece, piece), piece)

    def go_right(j, q):
        return remote(right_buf.at[j, q], right_buf.at[j, q], r_send.at[j, q], r_recv.at[j, q], space=after)

    def go_left(j, q):
        return remote(left_buf.at[j, q], left_buf.at[j, q], l_send.at[j, q], l_recv.at[j, q], space=before)

    def slot(j, q):
        return total.at[rows_of(q), pl.ds(pl.multiple_of(block_of(j) * width, width), width)]

    def final_right(j, q):
        return remote(slot(j, q), slot(j, q), fr_send.at[j, q], f_recv.at[j, q], space=after)

    def final_left(j, q):
        return remote(slot(j, q), slot(j, q), fl_send.at[j, q], f_recv.at[j, q], space=before)

    def step_right(j, q):
        @pl.when(jnp.logical_and(space < q, has_left))
        def _():
            go_right(j, q).wait_recv()
            right_buf[j, q] = (right_buf[j, q].astype(F32) + part[j, rows_of(q), :]).astype(BF16)

        @pl.when(jnp.logical_and(space < q, jnp.logical_not(has_left)))
        def _():
            right_buf[j, q] = part[j, rows_of(q), :].astype(BF16)

        @pl.when(space < q)
        def _():
            go_right(j, q).start()

    def step_left(j, q):
        @pl.when(jnp.logical_and(space > q, has_right))
        def _():
            go_left(j, q).wait_recv()
            left_buf[j, q] = (left_buf[j, q].astype(F32) + part[j, rows_of(q), :]).astype(BF16)

        @pl.when(jnp.logical_and(space > q, jnp.logical_not(has_right)))
        def _():
            left_buf[j, q] = part[j, rows_of(q), :].astype(BF16)

        @pl.when(space > q)
        def _():
            go_left(j, q).start()

    def each(count, body):
        def run(i, carry):
            body(i)
            return carry

        lax.fori_loop(0, count, run, 0)

    def reduce_pass(j):
        def body(m):
            step_right(j, own_count - 1 - m)
            step_left(j, m)

        each(own_count, body)

    def finish(j):
        @pl.when(space < own_count)
        def _():
            q = space

            @pl.when(has_left)
            def _():
                go_right(j, q).wait_recv()
                part[j, rows_of(q), :] = part[j, rows_of(q), :] + right_buf[j, q].astype(F32)

            @pl.when(has_right)
            def _():
                go_left(j, q).wait_recv()
                part[j, rows_of(q), :] = part[j, rows_of(q), :] + left_buf[j, q].astype(F32)

            slot(j, q)[...] = part[j, rows_of(q), :].astype(BF16)

            @pl.when(has_right)
            def _():
                final_right(j, q).start()

            @pl.when(has_left)
            def _():
                final_left(j, q).start()

    def share(j):
        def body(m):
            low = space - 1 - m

            @pl.when(jnp.logical_and(low >= 0, low < own_count))
            def _():
                final_right(j, low).wait_recv()

                @pl.when(has_right)
                def _():
                    final_right(j, low).start()

            high = space + 1 + m

            @pl.when(high < own_count)
            def _():
                final_left(j, high).wait_recv()

                @pl.when(has_left)
                def _():
                    final_left(j, high).start()

        each(n_s - 1, body)

    def drain(j):
        def body(q):
            @pl.when(space < q)
            def _():
                go_right(j, q).wait_send()

            @pl.when(space > q)
            def _():
                go_left(j, q).wait_send()

            @pl.when(jnp.logical_and(space >= q, has_right))
            def _():
                final_right(j, q).wait_send()

            @pl.when(jnp.logical_and(space <= q, has_left))
            def _():
                final_left(j, q).wait_send()

        each(own_count, body)

    def give(k):
        return remote(d_send.at[chan_rows(k)], d_recv.at[k], d_ssem.at[k], d_rsem.at[k], chan=flip(chan, k, n_c))

    def input_grad():
        weight_copy.wait()
        for i in range(0, in_all, width):
            for a in reversed(range(first, 3)):
                at = (a - first) * 9 * out_part
                skip, used = (2 - a) * plane, (frames - 2 + a) * plane
                value = tn(w_ref[at : at + 9 * out_part, i : i + width], xd[:, skip:cells])
                if a < 2:
                    value = value + d_acc[i : i + width, 0:used]
                d_acc[i : i + width, 0:used] = value
            d_send[i : i + width, :] = d_acc[i : i + width, :].astype(BF16)
        for k in range(1, n_c):
            give(k).start()

    def input_grad_end():
        for k in range(1, n_c):
            give(k).wait_recv()
        for t in range(frames):
            for h in range(rows):
                at = (t * rows + h) * cols
                value = d_acc[my_rows, at : at + cols]
                for k in range(1, n_c):
                    value = value + d_recv[k, :, at : at + cols].astype(F32)
                v = x_ref[t, h].astype(F32)
                s = jax.nn.sigmoid(v)
                gi_ref[t, h] = (value * (s * (1.0 + v * (1.0 - s)))).astype(BF16)

    for j in range(blocks + 2):
        if j < blocks:
            settle(j)
            kernel_grad(j)
            reduce_pass(j)
        if j == 0:
            input_grad()
        if j + 1 < blocks:
            fetch(j + 1)
        if 1 <= j < blocks + 1:
            finish(j - 1)
        if j >= 2:
            share(j - 2)
    input_grad_end()
    gw_ref[...] = total[...]

    @pl.when(has_right)
    def _():
        down().wait_send()
        down_sib().wait_send()

    @pl.when(has_left)
    def _():
        up().wait_send()
        up_sib().wait_send()

    across().wait_send()
    for k in range(n_c):
        relay(k).wait_send()
        if k:
            spread(k).wait_send()
            give(k).wait_send()
    for j in range(blocks):
        drain(j)


def on_device(sizes, inputs, grad_out, weight):
    n_c, n_s = sizes
    _, frames, rows, in_part, cols = inputs.shape
    out_part = grad_out.shape[3]
    in_all = weight.shape[4]
    cfg = (n_c, n_s, frames, rows, in_part, out_part, cols, in_all)
    half = out_part // 2
    first = max(0, 3 - frames)
    taps = 3 - first
    cells = frames * rows * cols
    width = max(LANES, in_part)
    blocks = in_all // width
    grad_rows = taps * 9 * half
    own_count = max(n for n in range(1, n_s + 1) if grad_rows % (16 * n) == 0)
    piece = grad_rows // own_count
    dma = pltpu.SemaphoreType.DMA
    chunk_sem = dma((blocks, own_count))
    vmem = pl.BlockSpec(memory_space=pltpu.VMEM)
    grad_in, total = pl.pallas_call(
        functools.partial(kernel, cfg),
        out_shape=(
            jax.ShapeDtypeStruct((frames, rows, in_part, cols), BF16),
            jax.ShapeDtypeStruct((grad_rows, in_all), BF16),
        ),
        in_specs=[vmem, vmem, pl.BlockSpec(memory_space=pl.ANY)],
        out_specs=(vmem, vmem),
        scratch_shapes=[
            pltpu.VMEM((2, in_all, cells), BF16),
            pltpu.VMEM((frames, out_part, cols), BF16),
            pltpu.VMEM((frames, out_part, cols), BF16),
            pltpu.VMEM((frames, half, cols), BF16),
            pltpu.VMEM((frames, half, cols), BF16),
            pltpu.VMEM((frames, rows, half, cols), BF16),
            pltpu.VMEM((9 * out_part, cells), BF16),
            pltpu.VMEM((2, 9 * half, cells), BF16),
            pltpu.VMEM((taps * 9 * out_part, in_all), BF16),
            pltpu.VMEM((blocks, grad_rows, width), F32),
            pltpu.VMEM((blocks, own_count, piece, width), BF16),
            pltpu.VMEM((blocks, own_count, piece, width), BF16),
            pltpu.VMEM((grad_rows, in_all), BF16),
            pltpu.VMEM((in_all, cells), F32),
            pltpu.VMEM((in_all, cells), BF16),
            pltpu.VMEM((n_c, in_part, cells), BF16),
            dma,
            dma((5,)),
            dma((5,)),
            dma((n_c,)),
            dma((n_c,)),
            dma((n_c,)),
            dma((n_c,)),
            chunk_sem, chunk_sem, chunk_sem, chunk_sem, chunk_sem, chunk_sem, chunk_sem,
            dma((n_c,)),
            dma((n_c,)),
        ],
        compiler_params=pltpu.CompilerParams(
            collective_id=0, has_side_effects=True, vmem_limit_bytes=48 << 20
        ),
    )(
        inputs.reshape(frames, rows, in_part, cols),
        grad_out.reshape(frames, rows, out_part, cols),
        weight.reshape(27 * out_part, in_all),
    )
    scaled = total.astype(F32) * (1.0 / 256.0)
    grad_weight = jnp.pad(
        scaled.reshape(taps, 3, 3, half, in_all), ((first, 0), (0, 0), (0, 0), (0, 0), (0, 0))
    )
    return grad_in.reshape(inputs.shape), grad_weight


def solution(mesh):
    return jax.shard_map(
        functools.partial(on_device, (mesh.shape["chan"], mesh.shape["space"])),
        mesh=mesh,
        in_specs=(
            P("rep", None, "space", "chan", None),
            P("rep", None, "space", "chan", None),
            P(None, None, None, "chan", None),
        ),
        out_specs=(
            P("rep", None, "space", "chan", None),
            P(None, None, None, ("chan", "rep"), None),
        ),
        check_vma=False,
    )
```

time: 260 us -> 91.2 us (0.35)
  waiting for transfers between devices: 187 us -> 0 us
  Pallas kernels: 0 us -> 83.2 us
  local copies, waits for them, and re-layouts: 26.3 us -> 6.83 us
  matrix products: 14.2 us -> 0 us
  between operations: 14 us -> 0.66 us
  other arithmetic: 9.39 us -> 0.32 us
  starting transfers between devices: 7.63 us -> 0 us
    psum x1 -> x0, waiting for transfers between devices: 132 us -> none  [on_device(): summed = lax.psum(clip_summed, 'space')]
    pallas_call x0 -> x1, Pallas kernels: none -> 83.2 us  [on_device(): pl.pallas_call(functools.partial(kernel, cfg), out_shape=(jax.ShapeDtypeS...]
    reduce_scatter x2 -> x0, waiting for transfers between devices: 46.4 us -> none  [the longest x1 38.5 us: on_device(): lax.psum_scatter(partial_value, 'chan', scatter_dimension=3, tiled=True)]
    dot_general x2 -> x0, matrix products: 14.2 us -> none  [the longest x1 7.54 us: on_device(): jnp.einsum('cthkw,ki->cthiw', stacked, flat_kernel, preferred_element_typ...]
    dot_general x2 -> x0, local copies, waits for them, and re-layouts: 14 us -> none  [on_device(): jnp.einsum('cthkw,cthiw->ki', stacked, activated, preferred_element_type=...]
    all_gather x1 -> x0, waiting for transfers between devices: 8.09 us -> none  [on_device(): gathered = lax.all_gather(inputs, 'chan', axis=3, tiled=True)]
    ppermute x2 -> x0, starting transfers between devices: 7.47 us -> none  [the longest x1 6.19 us: with_halo(): lax.ppermute(tail, axis, [(i, (i + 1) % count) for i in range(ends)])]
    unnamed x33 -> x7, local copies, waits for them, and re-layouts: 10.7 us -> 4.6 us
  transfers between devices with their start and end apart: 6 -> 0, of which waited for: 5 -> 0; matrix products, arithmetic and copies ran while one was open for 11% -> 0% of each run, Pallas kernels for 0% -> 0%
where the time goes in v1:
time: 91.2 us; the launch traced here: 91 us
  Pallas kernels  83.2 us (91%)
  local copies, waits for them, and re-layouts  6.83 us (7%)
    pallas_call x1, Pallas kernels, on_device(): pl.pallas_call(functools.partial(kernel, cfg), out_shape=(jax.ShapeDtypeS...  83.2 us
    unnamed x7, local copies, waits for them, and re-layouts  4.6 us
    pad x1, local copies, waits for them, and re-layouts, on_device(): jnp.pad(scaled.reshape(taps, 3, 3, half, in_all), ((first, 0), (0, 0), (0...  2.23 us

profile of v1, /device:TPU:0, one launch (start us, length us, event | category | flops | bytes accessed | tf_op | source)
XLA Modules:
  0.0 91.0 jit_solution(16498590258205437447)
XLA Ops:
  0.6 0.0 copy-start
  0.6 2.0 %copy-done = bf16[3,3,3,128,512]{4,3,2,1,0:T(8,128)(2,1)S(1)} copy-done((bf16[3,3,3,128,512]{4,3,2,1,0:T(8,128)(2,1)S(1)}, bf16[3,3,3,128,512]{4,3,2,1,0:T(8,128)(2,1)}, u32[]{:S(2)}) %copy-start) | copy-done | bytes 3538968
  2.6 0.0 copy-start.1
  2.6 0.9 %copy-done.1 = bf16[1,2,4,128,128]{4,3,2,1,0:T(8,128)(2,1)S(1)} copy-done((bf16[1,2,4,128,128]{4,3,2,1,0:T(8,128)(2,1)S(1)}, bf16[1,2,4,128,128]{4,3,2,1,0:T(8,128)(2,1)}, u32[]{:S(2)}) %copy-start.1) | copy-done | bytes 262168
  3.6 0.0 copy-start.2
  3.6 0.9 %copy-done.2 = bf16[1,2,4,128,128]{4,3,2,1,0:T(8,128)(2,1)S(1)} copy-done((bf16[1,2,4,128,128]{4,3,2,1,0:T(8,128)(2,1)S(1)}, bf16[1,2,4,128,128]{4,3,2,1,0:T(8,128)(2,1)}, u32[]{:S(2)}) %copy-start.2) | copy-done | bytes 262168
  4.5 83.2 %shard_map.50 = (bf16[2,4,128,128]{3,2,1,0:T(8,128)(2,1)S(1)}, bf16[1152,512]{1,0:T(8,128)(2,1)S(1)}) custom-call(bf16[2,4,128,128]{3,2,1,0:T(8,128)(2,1)S(1)} %bitcast.6, bf16[2,4,128,128]{3,2,1,0:T(8,128)(2,1)S(1)} %bitcast.7, bf16[3456,512]{1,0:T(8,128)(2,1)S(1)} %bitcast.5), custom_call_target="tpu_custom_call" | custom-call | tf_op jit(solution)/shard_map/pallas_call | solution.py:443
  87.8 0.3 convert_multiply_fusion
  88.1 2.2 %pad.4 = f32[3,3,3,64,512]{4,3,2,1,0:T(8,128)} pad(f32[2,3,3,64,512]{4,3,2,1,0:T(8,128)S(1)} %bitcast.9, f32[]{:T(128)} %constant.4.clone.1), padding=1_0x0_0x0_0x0_0x0_0 | pad | bytes 5898244 | tf_op jit(solution)/shard_map/jit(_pad)/pad | solution.py:488
  90.3 0.7 copy.6
Async XLA Ops:
  0.6 2.0 %copy-start = (bf16[3,3,3,128,512]{4,3,2,1,0:T(8,128)(2,1)S(1)}, bf16[3,3,3,128,512]{4,3,2,1,0:T(8,128)(2,1)}, u32[]{:S(2)}) copy-start(bf16[3,3,3,128,512]{4,3,2,1,0:T(8,128)(2,1)} %param.5) | copy-start | bytes 10616836
  2.6 0.9 %copy-start.1 = (bf16[1,2,4,128,128]{4,3,2,1,0:T(8,128)(2,1)S(1)}, bf16[1,2,4,128,128]{4,3,2,1,0:T(8,128)(2,1)}, u32[]{:S(2)}) copy-start(bf16[1,2,4,128,128]{4,3,2,1,0:T(8,128)(2,1)} %param.3) | copy-start | bytes 786436
  3.6 0.9 %copy-start.2 = (bf16[1,2,4,128,128]{4,3,2,1,0:T(8,128)(2,1)S(1)}, bf16[1,2,4,128,128]{4,3,2,1,0:T(8,128)(2,1)}, u32[]{:S(2)}) copy-start(bf16[1,2,4,128,128]{4,3,2,1,0:T(8,128)(2,1)} %param.4) | copy-start | bytes 786436

commit v2 on v1

--- a/solution.py
+++ b/solution.py
@@ -11,6 +11,7 @@
 F32 = jnp.float32
 BF16 = jnp.bfloat16
 LANES = 128
+SPLIT = 2
 
 
 def flip(index, mask, count):
@@ -19,6 +20,13 @@
         out = out + (((index // bit) + ((mask // bit) % 2)) % 2) * bit
         bit *= 2
     return out
+
+
+def cut(grad_rows, n_s):
+    split = max(n for n in range(1, SPLIT + 1) if grad_rows % (16 * n) == 0)
+    share = grad_rows // split
+    count = max(n for n in range(1, n_s + 1) if share % (16 * n) == 0)
+    return split, count, share // count
 
 
 def nt(a, b):
@@ -49,8 +57,8 @@
     blocks = in_all // width
     per = width // in_part
     grad_rows = taps * 9 * half
-    own_count = max(n for n in range(1, n_s + 1) if grad_rows % (16 * n) == 0)
-    piece = grad_rows // own_count
+    split, own_count, piece = cut(grad_rows, n_s)
+    units = blocks * split
 
     chan = lax.axis_index("chan")
     space = lax.axis_index("space")
@@ -227,51 +235,28 @@
         for k in range(j * per, (j + 1) * per):
             relay(k).wait_recv()
 
-    def rows_of(q):
-        return pl.ds(pl.multiple_of(q * piece, piece), piece)
-
-    def go_right(j, q):
-        return remote(right_buf.at[j, q], right_buf.at[j, q], r_send.at[j, q], r_recv.at[j, q], space=after)
-
-    def go_left(j, q):
-        return remote(left_buf.at[j, q], left_buf.at[j, q], l_send.at[j, q], l_recv.at[j, q], space=before)
-
-    def slot(j, q):
-        return total.at[rows_of(q), pl.ds(pl.multiple_of(block_of(j) * width, width), width)]
-
-    def final_right(j, q):
-        return remote(slot(j, q), slot(j, q), fr_send.at[j, q], f_recv.at[j, q], space=after)
-
-    def final_left(j, q):
-        return remote(slot(j, q), slot(j, q), fl_send.at[j, q], f_recv.at[j, q], space=before)
-
-    def step_right(j, q):
-        @pl.when(jnp.logical_and(space < q, has_left))
-        def _():
-            go_right(j, q).wait_recv()
-            right_buf[j, q] = (right_buf[j, q].astype(F32) + part[j, rows_of(q), :]).astype(BF16)
-
-        @pl.when(jnp.logical_and(space < q, jnp.logical_not(has_left)))
-        def _():
-            right_buf[j, q] = part[j, rows_of(q), :].astype(BF16)
-
-        @pl.when(space < q)
-        def _():
-            go_right(j, q).start()
-
-    def step_left(j, q):
-        @pl.when(jnp.logical_and(space > q, has_right))
-        def _():
-            go_left(j, q).wait_recv()
-            left_buf[j, q] = (left_buf[j, q].astype(F32) + part[j, rows_of(q), :]).astype(BF16)
-
-        @pl.when(jnp.logical_and(space > q, jnp.logical_not(has_right)))
-        def _():
-            left_buf[j, q] = part[j, rows_of(q), :].astype(BF16)
-
-        @pl.when(space > q)
-        def _():
-            go_left(j, q).start()
+    def rows_of(u, q):
+        return pl.ds(pl.multiple_of(((u % split) * own_count + q) * piece, piece), piece)
+
+    def own(u, q):
+        return part[u // split, rows_of(u, q), :]
+
+    def go_right(u, q):
+        return remote(right_buf.at[u, q], right_buf.at[u, q], r_send.at[u, q], r_recv.at[u, q], space=after)
+
+    def go_left(u, q):
+        return remote(left_buf.at[u, q], left_buf.at[u, q], l_send.at[u, q], l_recv.at[u, q], space=before)
+
+    def slot(u, q):
+        return total.at[
+            rows_of(u, q), pl.ds(pl.multiple_of(block_of(u // split) * width, width), width)
+        ]
+
+    def final_right(u, q):
+        return remote(slot(u, q), slot(u, q), fr_send.at[u, q], f_recv.at[u, q], space=after)
+
+    def final_left(u, q):
+        return remote(slot(u, q), slot(u, q), fl_send.at[u, q], f_recv.at[u, q], space=before)
 
     def each(count, body):
         def run(i, carry):
@@ -280,79 +265,117 @@
 
         lax.fori_loop(0, count, run, 0)
 
-    def reduce_pass(j):
-        def body(m):
-            step_right(j, own_count - 1 - m)
-            step_left(j, m)
-
-        each(own_count, body)
-
-    def finish(j):
-        @pl.when(space < own_count)
-        def _():
-            q = space
-
-            @pl.when(has_left)
-            def _():
-                go_right(j, q).wait_recv()
-                part[j, rows_of(q), :] = part[j, rows_of(q), :] + right_buf[j, q].astype(F32)
-
-            @pl.when(has_right)
-            def _():
-                go_left(j, q).wait_recv()
-                part[j, rows_of(q), :] = part[j, rows_of(q), :] + left_buf[j, q].astype(F32)
-
-            slot(j, q)[...] = part[j, rows_of(q), :].astype(BF16)
-
-            @pl.when(has_right)
-            def _():
-                final_right(j, q).start()
-
-            @pl.when(has_left)
-            def _():
-                final_left(j, q).start()
-
-    def share(j):
-        def body(m):
-            low = space - 1 - m
-
-            @pl.when(jnp.logical_and(low >= 0, low < own_count))
-            def _():
-                final_right(j, low).wait_recv()
+    def live(u):
+        return jnp.logical_and(u >= 0, u < units)
+
+    def step_right(u, q):
+        @pl.when(has_left)
+        def _():
+            go_right(u, q).wait_recv()
+            right_buf[u, q] = (right_buf[u, q].astype(F32) + own(u, q)).astype(BF16)
+
+        @pl.when(jnp.logical_not(has_left))
+        def _():
+            right_buf[u, q] = own(u, q).astype(BF16)
+
+        go_right(u, q).start()
+
+    def step_left(u, q):
+        @pl.when(has_right)
+        def _():
+            go_left(u, q).wait_recv()
+            left_buf[u, q] = (left_buf[u, q].astype(F32) + own(u, q)).astype(BF16)
+
+        @pl.when(jnp.logical_not(has_right))
+        def _():
+            left_buf[u, q] = own(u, q).astype(BF16)
+
+        go_left(u, q).start()
+
+    def finish(u, q):
+        @pl.when(has_left)
+        def _():
+            go_right(u, q).wait_recv()
+            part[u // split, rows_of(u, q), :] = own(u, q) + right_buf[u, q].astype(F32)
+
+        @pl.when(has_right)
+        def _():
+            go_left(u, q).wait_recv()
+            part[u // split, rows_of(u, q), :] = own(u, q) + left_buf[u, q].astype(F32)
+
+        slot(u, q)[...] = own(u, q).astype(BF16)
+
+        @pl.when(has_right)
+        def _():
+            final_right(u, q).start()
+
+        @pl.when(has_left)
+        def _():
+            final_left(u, q).start()
+
+    def settled(q):
+        return jnp.maximum(q, n_s - 1 - q)
+
+    def tick(time):
+        right_unit = time - space
+        left_unit = time - (n_s - 1 - space)
+
+        def reduce(m):
+            far = own_count - 1 - m
+
+            @pl.when(jnp.logical_and(space < far, live(right_unit)))
+            def _():
+                step_right(right_unit, far)
+
+            @pl.when(jnp.logical_and(space > m, live(left_unit)))
+            def _():
+                step_left(left_unit, m)
+
+        each(own_count, reduce)
+        done_unit = time - settled(space)
+
+        @pl.when(jnp.logical_and(space < own_count, live(done_unit)))
+        def _():
+            finish(done_unit, space)
+
+        def share(q):
+            unit = time - settled(q) - jnp.maximum(space - q, q - space)
+
+            @pl.when(jnp.logical_and(q < space, live(unit)))
+            def _():
+                final_right(unit, q).wait_recv()
 
                 @pl.when(has_right)
                 def _():
-                    final_right(j, low).start()
-
-            high = space + 1 + m
-
-            @pl.when(high < own_count)
-            def _():
-                final_left(j, high).wait_recv()
+                    final_right(unit, q).start()
+
+            @pl.when(jnp.logical_and(q > space, live(unit)))
+            def _():
+                final_left(unit, q).wait_recv()
 
                 @pl.when(has_left)
                 def _():
-                    final_left(j, high).start()
-
-        each(n_s - 1, body)
-
-    def drain(j):
+                    final_left(unit, q).start()
+
+        each(own_count, share)
+
+    def drain(u):
         def body(q):
             @pl.when(space < q)
             def _():
-                go_right(j, q).wait_send()
+                go_right(u, q).wait_send()
 
             @pl.when(space > q)
             def _():
-                go_left(j, q).wait_send()
+                go_left(u, q).wait_send()
 
             @pl.when(jnp.logical_and(space >= q, has_right))
             def _():
-                final_right(j, q).wait_send()
+                final_right(u, q).wait_send()
 
             @pl.when(jnp.logical_and(space <= q, has_left))
             def _():
-                final_left(j, q).wait_send()
+                final_left(u, q).wait_send()
 
         each(own_count, body)
 
@@ -386,19 +409,15 @@
                 s = jax.nn.sigmoid(v)
                 gi_ref[t, h] = (value * (s * (1.0 + v * (1.0 - s)))).astype(BF16)
 
-    for j in range(blocks + 2):
-        if j < blocks:
-            settle(j)
-            kernel_grad(j)
-            reduce_pass(j)
+    for j in range(blocks):
+        settle(j)
+        kernel_grad(j)
+        each(split, lambda i: tick(j * split + i))
         if j == 0:
             input_grad()
         if j + 1 < blocks:
             fetch(j + 1)
-        if 1 <= j < blocks + 1:
-            finish(j - 1)
-        if j >= 2:
-            share(j - 2)
+    each(2 * n_s - 2, lambda i: tick(units + i))
     input_grad_end()
     gw_ref[...] = total[...]
 
@@ -418,8 +437,7 @@
         if k:
             spread(k).wait_send()
             give(k).wait_send()
-    for j in range(blocks):
-        drain(j)
+    each(units, drain)
 
 
 def on_device(sizes, inputs, grad_out, weight):
@@ -435,10 +453,10 @@
     width = max(LANES, in_part)
     blocks = in_all // width
     grad_rows = taps * 9 * half
-    own_count = max(n for n in range(1, n_s + 1) if grad_rows % (16 * n) == 0)
-    piece = grad_rows // own_count
+    split, own_count, piece = cut(grad_rows, n_s)
+    units = blocks * split
     dma = pltpu.SemaphoreType.DMA
-    chunk_sem = dma((blocks, own_count))
+    chunk_sem = dma((units, own_count))
     vmem = pl.BlockSpec(memory_space=pltpu.VMEM)
     grad_in, total = pl.pallas_call(
         functools.partial(kernel, cfg),
@@ -459,8 +477,8 @@
             pltpu.VMEM((2, 9 * half, cells), BF16),
             pltpu.VMEM((taps * 9 * out_part, in_all), BF16),
             pltpu.VMEM((blocks, grad_rows, width), F32),
-            pltpu.VMEM((blocks, own_count, piece, width), BF16),
-            pltpu.VMEM((blocks, own_count, piece, width), BF16),
+            pltpu.VMEM((units, own_count, piece, width), BF16),
+            pltpu.VMEM((units, own_count, piece, width), BF16),
             pltpu.VMEM((grad_rows, in_all), BF16),
             pltpu.VMEM((in_all, cells), F32),
             pltpu.VMEM((in_all, cells), BF16),

time: 91.2 us -> 68 us (0.75)
  Pallas kernels: 83.2 us -> 60 us
    pallas_call x1, Pallas kernels: 83.2 us -> 60 us  [on_device(): pl.pallas_call(functools.partial(kernel, cfg), out_shape=(jax.ShapeDtypeS...]
where the time goes in v2:
time: 68 us; the launch traced here: 67.8 us
  Pallas kernels  60 us (88%)
  local copies, waits for them, and re-layouts  6.83 us (10%)
    pallas_call x1, Pallas kernels, on_device(): pl.pallas_call(functools.partial(kernel, cfg), out_shape=(jax.ShapeDtypeS...  60 us
    unnamed x7, local copies, waits for them, and re-layouts  4.6 us
    pad x1, local copies, waits for them, and re-layouts, on_device(): jnp.pad(scaled.reshape(taps, 3, 3, half, in_all), ((first, 0), (0, 0), (0...  2.23 us

profile of v2, /device:TPU:0, one launch (start us, length us, event | category | flops | bytes accessed | tf_op | source)
XLA Modules:
  0.0 67.8 jit_solution(4699737117358695596)
XLA Ops:
  0.6 0.0 copy-start
  0.6 2.0 %copy-done = bf16[3,3,3,128,512]{4,3,2,1,0:T(8,128)(2,1)S(1)} copy-done((bf16[3,3,3,128,512]{4,3,2,1,0:T(8,128)(2,1)S(1)}, bf16[3,3,3,128,512]{4,3,2,1,0:T(8,128)(2,1)}, u32[]{:S(2)}) %copy-start) | copy-done | bytes 3538968
  2.6 0.0 copy-start.1
  2.6 0.9 %copy-done.1 = bf16[1,2,4,128,128]{4,3,2,1,0:T(8,128)(2,1)S(1)} copy-done((bf16[1,2,4,128,128]{4,3,2,1,0:T(8,128)(2,1)S(1)}, bf16[1,2,4,128,128]{4,3,2,1,0:T(8,128)(2,1)}, u32[]{:S(2)}) %copy-start.1) | copy-done | bytes 262168
  3.6 0.0 copy-start.2
  3.6 0.9 %copy-done.2 = bf16[1,2,4,128,128]{4,3,2,1,0:T(8,128)(2,1)S(1)} copy-done((bf16[1,2,4,128,128]{4,3,2,1,0:T(8,128)(2,1)S(1)}, bf16[1,2,4,128,128]{4,3,2,1,0:T(8,128)(2,1)}, u32[]{:S(2)}) %copy-start.2) | copy-done | bytes 262168
  4.5 60.0 %shard_map.50 = (bf16[2,4,128,128]{3,2,1,0:T(8,128)(2,1)S(1)}, bf16[1152,512]{1,0:T(8,128)(2,1)S(1)}) custom-call(bf16[2,4,128,128]{3,2,1,0:T(8,128)(2,1)S(1)} %bitcast.6, bf16[2,4,128,128]{3,2,1,0:T(8,128)(2,1)S(1)} %bitcast.7, bf16[3456,512]{1,0:T(8,128)(2,1)S(1)} %bitcast.5), custom_call_target="tpu_custom_call" | custom-call | tf_op jit(solution)/shard_map/pallas_call | solution.py:461
  64.5 0.3 convert_multiply_fusion
  64.9 2.2 %pad.4 = f32[3,3,3,64,512]{4,3,2,1,0:T(8,128)} pad(f32[2,3,3,64,512]{4,3,2,1,0:T(8,128)S(1)} %bitcast.9, f32[]{:T(128)} %constant.4.clone.1), padding=1_0x0_0x0_0x0_0x0_0 | pad | bytes 5898244 | tf_op jit(solution)/shard_map/jit(_pad)/pad | solution.py:506
  67.1 0.7 %copy.6 = bf16[1,2,4,128,128]{4,3,2,1,0:T(8,128)(2,1)} copy(bf16[1,2,4,128,128]{4,3,2,1,0:T(8,128)(2,1)S(1)} %bitcast.8) | data formatting | bytes 524288
Async XLA Ops:
  0.6 2.0 %copy-start = (bf16[3,3,3,128,512]{4,3,2,1,0:T(8,128)(2,1)S(1)}, bf16[3,3,3,128,512]{4,3,2,1,0:T(8,128)(2,1)}, u32[]{:S(2)}) copy-start(bf16[3,3,3,128,512]{4,3,2,1,0:T(8,128)(2,1)} %param.5) | copy-start | bytes 10616836
  2.6 0.9 %copy-start.1 = (bf16[1,2,4,128,128]{4,3,2,1,0:T(8,128)(2,1)S(1)}, bf16[1,2,4,128,128]{4,3,2,1,0:T(8,128)(2,1)}, u32[]{:S(2)}) copy-start(bf16[1,2,4,128,128]{4,3,2,1,0:T(8,128)(2,1)} %param.3) | copy-start | bytes 786436
  3.6 0.9 %copy-start.2 = (bf16[1,2,4,128,128]{4,3,2,1,0:T(8,128)(2,1)S(1)}, bf16[1,2,4,128,128]{4,3,2,1,0:T(8,128)(2,1)}, u32[]{:S(2)}) copy-start(bf16[1,2,4,128,128]{4,3,2,1,0:T(8,128)(2,1)} %param.4) | copy-start | bytes 786436

commit v3 on v2

--- a/solution.py
+++ b/solution.py
@@ -11,7 +11,7 @@
 F32 = jnp.float32
 BF16 = jnp.bfloat16
 LANES = 128
-SPLIT = 2
+SPLIT = 3
 
 
 def flip(index, mask, count):

time: 68 us -> 76.1 us (1.12)
  Pallas kernels: 60 us -> 68.1 us
    pallas_call x1, Pallas kernels: 60 us -> 68.1 us  [on_device(): pl.pallas_call(functools.partial(kernel, cfg), out_shape=(jax.ShapeDtypeS...]
where the time goes in v3:
time: 76.1 us; the launch traced here: 75.9 us
  Pallas kernels  68.1 us (89%)
  local copies, waits for them, and re-layouts  6.83 us (9%)
    pallas_call x1, Pallas kernels, on_device(): pl.pallas_call(functools.partial(kernel, cfg), out_shape=(jax.ShapeDtypeS...  68.1 us
    unnamed x7, local copies, waits for them, and re-layouts  4.6 us
    pad x1, local copies, waits for them, and re-layouts, on_device(): jnp.pad(scaled.reshape(taps, 3, 3, half, in_all), ((first, 0), (0, 0), (0...  2.23 us

profile of v3, /device:TPU:0, one launch (start us, length us, event | category | flops | bytes accessed | tf_op | source)
XLA Modules:
  0.0 75.9 jit_solution(5574387965343049323)
XLA Ops:
  0.6 0.0 copy-start
  0.6 2.0 %copy-done = bf16[3,3,3,128,512]{4,3,2,1,0:T(8,128)(2,1)S(1)} copy-done((bf16[3,3,3,128,512]{4,3,2,1,0:T(8,128)(2,1)S(1)}, bf16[3,3,3,128,512]{4,3,2,1,0:T(8,128)(2,1)}, u32[]{:S(2)}) %copy-start) | copy-done | bytes 3538968
  2.6 0.0 copy-start.1
  2.6 0.9 %copy-done.1 = bf16[1,2,4,128,128]{4,3,2,1,0:T(8,128)(2,1)S(1)} copy-done((bf16[1,2,4,128,128]{4,3,2,1,0:T(8,128)(2,1)S(1)}, bf16[1,2,4,128,128]{4,3,2,1,0:T(8,128)(2,1)}, u32[]{:S(2)}) %copy-start.1) | copy-done | bytes 262168
  3.6 0.0 copy-start.2
  3.6 0.9 %copy-done.2 = bf16[1,2,4,128,128]{4,3,2,1,0:T(8,128)(2,1)S(1)} copy-done((bf16[1,2,4,128,128]{4,3,2,1,0:T(8,128)(2,1)S(1)}, bf16[1,2,4,128,128]{4,3,2,1,0:T(8,128)(2,1)}, u32[]{:S(2)}) %copy-start.2) | copy-done | bytes 262168
  4.5 68.1 %shard_map.50 = (bf16[2,4,128,128]{3,2,1,0:T(8,128)(2,1)S(1)}, bf16[1152,512]{1,0:T(8,128)(2,1)S(1)}) custom-call(bf16[2,4,128,128]{3,2,1,0:T(8,128)(2,1)S(1)} %bitcast.6, bf16[2,4,128,128]{3,2,1,0:T(8,128)(2,1)S(1)} %bitcast.7, bf16[3456,512]{1,0:T(8,128)(2,1)S(1)} %bitcast.5), custom_call_target="tpu_custom_call" | custom-call | tf_op jit(solution)/shard_map/pallas_call | solution.py:461
  72.6 0.3 convert_multiply_fusion
  72.9 2.2 %pad.4 = f32[3,3,3,64,512]{4,3,2,1,0:T(8,128)} pad(f32[2,3,3,64,512]{4,3,2,1,0:T(8,128)S(1)} %bitcast.9, f32[]{:T(128)} %constant.4.clone.1), padding=1_0x0_0x0_0x0_0x0_0 | pad | bytes 5898244 | tf_op jit(solution)/shard_map/jit(_pad)/pad | solution.py:506
  75.2 0.7 copy.6
Async XLA Ops:
  0.6 2.0 %copy-start = (bf16[3,3,3,128,512]{4,3,2,1,0:T(8,128)(2,1)S(1)}, bf16[3,3,3,128,512]{4,3,2,1,0:T(8,128)(2,1)}, u32[]{:S(2)}) copy-start(bf16[3,3,3,128,512]{4,3,2,1,0:T(8,128)(2,1)} %param.5) | copy-start | bytes 10616836
  2.6 0.9 %copy-start.1 = (bf16[1,2,4,128,128]{4,3,2,1,0:T(8,128)(2,1)S(1)}, bf16[1,2,4,128,128]{4,3,2,1,0:T(8,128)(2,1)}, u32[]{:S(2)}) copy-start(bf16[1,2,4,128,128]{4,3,2,1,0:T(8,128)(2,1)} %param.3) | copy-start | bytes 786436
  3.6 0.9 %copy-start.2 = (bf16[1,2,4,128,128]{4,3,2,1,0:T(8,128)(2,1)S(1)}, bf16[1,2,4,128,128]{4,3,2,1,0:T(8,128)(2,1)}, u32[]{:S(2)}) copy-start(bf16[1,2,4,128,128]{4,3,2,1,0:T(8,128)(2,1)} %param.4) | copy-start | bytes 786436
